TPU v7x, 256 devices: a whole 4x4x8 slice. The times are simulated.
256 devices in a mesh: batch: 4 (over z_lo, core), row: 4 (over x), col: 16 (over y, z_hi).
Axes of the slice: x: 4, y: 4, z: 8 (z_hi: 4, z_lo: 2; z = z_hi * 2 + z_lo), core: 2. Of those that a mesh axis runs over, the one named last changes fastest.
Arguments:
- embeddings: bfloat16 [512, 128, 512], P('batch', 'col', 'row'), may hold values from -170 to 170
- projection: bfloat16 [512, 32], replicated, may hold values from -0.25 to 0.25
- w_in: bfloat16 [16384, 2048], P('row', 'col'), may hold values from -0.046875 to 0.046875
- bias: float32 [2048], P('col'), may hold values from -3 to 3
- w_out: bfloat16 [2048, 128, 512], P(None, 'col', 'row'), may hold values from -0.125 to 0.125
- cotangent: bfloat16 [512, 128, 512], P('batch', 'col', 'row'), may hold values from -0.1796875 to 0.1796875
Outputs:
- mixed: bfloat16 [512, 128, 512], P('batch', 'col', 'row')
- grad_out: float32 [2048, 128, 512], P('batch', 'col', 'row')
- grad_in: float32 [16384, 2048], P('row', 'col')
- grad_bias: float32 [2048], P('col')
- grad_proj: float32 [512, 32], P('row')
All inputs are finite; a program needn't handle non-finite values.
Results may differ from a plain program's by a relative error of at most 0.006.
Values may be sent and summed in bfloat16 or wider, within the bound.
A program may use at most 128 MiB of HBM per device.

v0:
```python
import jax
import jax.numpy as jnp
from jax import lax
from jax.sharding import PartitionSpec as P

epsilon = 1e-06


def copy_for_each(array, axis):
    size = lax.axis_size(axis)
    return lax.all_to_all(
        jnp.broadcast_to(array[None], (size, *array.shape)), axis, 0, 0, tiled=True
    )


def of_everyone(array, axis):
    everything = copy_for_each(array, axis)
    return jnp.sum(everything, axis=0)


def joined_along(tiles, dim):
    tiles = jnp.moveaxis(tiles, 0, dim)
    lengths = tiles.shape
    return tiles.reshape(*lengths[:dim], lengths[dim] * lengths[dim + 1], *lengths[dim + 2 :])


def gathered_copies(array, axis, dim):
    return joined_along(copy_for_each(array, axis), dim)


def cut_along(array, dim, size):
    lengths = array.shape
    tiles = array.reshape(*lengths[:dim], size, lengths[dim] // size, *lengths[dim + 1 :])
    return jnp.moveaxis(tiles, dim, 0)


def sent_and_summed(array, axis, dim):
    size = lax.axis_size(axis)
    tiles = lax.all_to_all(cut_along(array, dim, size), axis, 0, 0, tiled=True)
    return jnp.sum(tiles, axis=0)


def in_one_piece(arrays, axis, dim, along):
    both = jnp.concatenate(arrays, axis=along)
    whole, at, gathered = (lax.all_gather(both, axis, axis=dim, tiled=True), 0, [])
    for a in arrays:
        gathered.append(lax.slice_in_dim(whole, at, at + a.shape[along], axis=along))
        at += a.shape[along]
    return tuple(gathered)


def filled_up(lines, size):
    spare = -lines.shape[0] % size
    if not spare:
        return lines
    return jnp.concatenate([lines, jnp.zeros((spare, *lines.shape[1:]), lines.dtype)])


def sum_by_parts(array, axis):
    lines = array.reshape(-1, *array.shape[1:][-1:])
    padded = filled_up(lines, lax.axis_size(axis))
    own = lax.psum_scatter(padded, axis, scatter_dimension=0, tiled=True)
    whole = lax.all_gather(own, axis, axis=0, tiled=True)
    return whole[: len(lines)].reshape(array.shape)


def contract_first(left, right):
    return lax.dot_general(
        left, right, (((0,), (0,)), ((), ())), preferred_element_type=jnp.float32
    )


def contract_last(left, right):
    return lax.dot_general(
        left, right, (((1,), (1,)), ((), ())), preferred_element_type=jnp.float32
    )


def local(embeddings, projection, w_in, bias, w_out, cotangent):
    highest = lax.Precision.HIGHEST
    tok_rows, feat_local, emb_local = embeddings.shape
    rank_cols = projection.shape[1]
    row_count = lax.axis_size("row")
    row_place = lax.axis_index("row")
    emb_float = embeddings.astype(jnp.float32)
    own_proj = lax.dynamic_slice_in_dim(projection, row_place * emb_local, emb_local, 0)
    folded = of_everyone(
        jnp.einsum("bde,ek->bdk", embeddings, own_proj, preferred_element_type=jnp.float32), "row"
    )
    partial_value = jnp.einsum("bde,bdk->bek", emb_float, folded, precision=highest)
    interact = lax.psum(partial_value, "col")
    feature_count = emb_local * row_count * rank_cols
    square_sum = of_everyone(jnp.sum(interact * interact, axis=(1, 2)), "row")
    inv_rms = lax.rsqrt(square_sum / feature_count + epsilon)[:, None, None]
    normed = interact * inv_rms
    activated = normed.astype(jnp.bfloat16).reshape(tok_rows, emb_local * rank_cols)
    preact = of_everyone(jnp.dot(activated, w_in, preferred_element_type=jnp.float32), "row") + bias
    hidden = jax.nn.silu(preact).astype(jnp.bfloat16)
    hidden_all = gathered_copies(hidden, "col", 1)
    flat_out = w_out.reshape(w_out.shape[0], feat_local * emb_local)
    mixed = (
        jnp.dot(hidden_all, flat_out, preferred_element_type=jnp.float32)
        .astype(jnp.bfloat16)
        .reshape(tok_rows, feat_local, emb_local)
    )
    cot_rows = cotangent.reshape(tok_rows, feat_local * emb_local)
    d_cols = sent_and_summed(contract_last(cot_rows, flat_out), "col", 1)
    d_hidden = of_everyone(d_cols, "row")
    sigmoid_pre = jax.nn.sigmoid(preact)
    d_preact = d_hidden * sigmoid_pre * (1.0 + preact * (1.0 - sigmoid_pre))
    d_pre_b = d_preact.astype(jnp.bfloat16)
    per_batch = w_out.shape[0] // lax.axis_size("batch")
    every_hidden, every_cot = in_one_piece((hidden_all, cot_rows), "batch", 0, 1)
    own_hidden = lax.dynamic_slice_in_dim(
        every_hidden, lax.axis_index("batch") * per_batch, per_batch, 1
    )
    grad_flat = contract_first(own_hidden, every_cot)
    grad_out = grad_flat.reshape(per_batch, feat_local, emb_local)
    grad_in, grad_bias = lax.psum(
        (contract_first(activated, d_pre_b), jnp.sum(d_preact, axis=0)), "batch"
    )
    d_act = sum_by_parts(contract_last(d_pre_b, w_in), "col").reshape(
        tok_rows, emb_local, rank_cols
    )
    inner_term = of_everyone(jnp.sum(d_act * normed, axis=(1, 2)), "row") / feature_count
    d_inter = (inv_rms * (d_act - normed * inner_term[:, None, None])).astype(jnp.bfloat16)
    back_fold = of_everyone(
        jnp.einsum("bek,bde->bdk", d_inter, embeddings, preferred_element_type=jnp.float32), "row"
    )
    grad_proj = of_everyone(
        jnp.einsum("bde,bdk->ek", emb_float, back_fold, precision=highest), ("batch", "col")
    )
    return (mixed, grad_out, grad_in, grad_bias, grad_proj)


def solution(mesh):
    placed = (
        P("batch", "col", "row"),
        P(),
        P("row", "col"),
        P("col"),
        P(None, "col", "row"),
        P("batch", "col", "row"),
    )
    return jax.shard_map(
        local,
        mesh=mesh,
        in_specs=placed,
        out_specs=(
            P("batch", "col", "row"),
            P("batch", "col", "row"),
            P("row", "col"),
            P("col"),
            P("row", None),
        ),
        check_vma=False,
    )
```

profile of v0, /device:TPU:1, one launch (start us, length us, event | category | flops | bytes accessed | tf_op | source)
XLA Modules:
  0.0 535.5 jit_solution(8240638500809765838)
XLA Ops:
  7.2 1.2 convolution_bitcast_fusion.4
  8.4 0.9 broadcast_in_dim.16
  9.3 4.8 all-to-all-start
  14.4 7.4 %dot_general.47 = bf16[16,128,1024]{2,1,0:T(8,128)(2,1)} reshape(bf16[2048,8,128]{2,1,0:T(8,128)(2,1)} %param.10) | data formatting | bytes 8388608 | tf_op jit(solution)/shard_map/dot_general | solution.py:74
  22.1 3.2 convolution_bitcast_fusion.1
  25.3 4.7 convolution_bitcast_fusion.2
  30.0 11.6 %all-to-all-start.4 = ((f32[16,128,128]{2,1,0:T(8,128)}), f32[16,128,128]{2,1,0:T(8,128)}, u32[]{:S(2)}, u32[]{:S(2)}) async-start(f32[16,128,128]{2,1,0:T(8,128)} %convolution_bitcast_fusion.2), calls=%async_computation.4 | async-start | bytes 2097152 | tf_op jit(solution)/shard_map/all_to_all | solution.py:39
  41.6 172.1 %all-reduce.3.cloned.1.call-done = f32[128,128,32]{1,2,0:T(8,128)} async-done(((f32[128,128,32]{1,2,0:T(8,128)}), f32[128,128,32]{1,2,0:T(8,128)}) %all-reduce.3.cloned.1.call-update) | async-done | bytes 2097168 | tf_op jit(solution)/shard_map/psum | solution.py:91
  213.7 2.8 multiply_reduce_fusion.1
  217.0 3.3 all-to-all-start.1
  220.3 1.3 reduce_sum.103
  221.6 2.8 all-to-all-done.1
  225.1 4.0 all-to-all-start.5
  229.2 1.2 multiply_convert_fusion.1
  230.4 3.3 copy.58
  233.7 1.7 fusion.24
  235.4 0.7 broadcast_in_dim.18
  236.1 4.2 all-to-all-start.2
  240.3 1.0 reduce_sum.104
  241.3 5.8 %all-to-all-done.2 = f32[4,128,128]{2,1,0:T(8,128)} async-done(((f32[4,128,128]{2,1,0:T(8,128)}), f32[4,128,128]{2,1,0:T(8,128)}, u32[]{:S(2)}, u32[]{:S(2)}) %all-to-all-start.2) | async-done | bytes 262176 | tf_op jit(solution)/shard_map/all_to_all | solution.py:11
  247.1 1.6 reduce_sum.102
  248.7 0.9 fusion.23
  249.6 1.8 fusion.15
  251.4 95.4 %reduce-scatter.2.cloned.1.call-done = f32[8,4096]{1,0:T(8,128)} async-done(((f32[128,4096]{1,0:T(8,128)}), f32[8,4096]{1,0:T(8,128)}) %reduce-scatter.2.cloned.1.call-update) | async-done | bytes 131088 | tf_op jit(solution)/shard_map/reduce_scatter | solution.py:62
  347.1 23.1 %all_to_all.47 = bf16[16,128,128]{1,2,0:T(8,128)(2,1)S(1)} all-to-all(bf16[16,128,128]{1,2,0:T(8,128)(2,1)S(1)} %broadcast_in_dim.19), channel_id=1, replica_groups=mesh['batch'=4,'row'=4,'col'=16] {'col'}, dimensions={0} | all-to-all | bytes 1048576 | tf_op jit(solution)/shard_map/all_to_all | solution.py:11
  370.2 0.8 copy-done.5
  371.0 1.9 pad_maximum_fusion
  372.9 34.7 %all-gather.5.cloned.1.call-done = f32[128,4096]{1,0:T(8,128)} async-done(((f32[8,4096]{1,0:T(8,128)}), f32[128,4096]{1,0:T(8,128)}) %all-gather.5.cloned.1.call-update) | async-done | bytes 2097168 | tf_op jit(solution)/shard_map/all_gather | solution.py:63
  407.6 2.9 copy.62
  410.5 3.4 copy.65
  413.9 3.5 multiply_reduce_fusion
  417.3 8.2 %all_to_all.48 = f32[4,1,128]{2,1,0:T(1,128)S(1)} all-to-all(f32[4,1,128]{2,1,0:T(1,128)S(1)} %broadcast_in_dim.21), channel_id=1, replica_groups=mesh['batch'=4,'row'=4,'col'=16] {'row'}, dimensions={0} | all-to-all | bytes 4096 | tf_op jit(solution)/shard_map/all_to_all | solution.py:11
  425.5 3.1 convolution_bitcast_fusion.3
  428.7 1.3 copy.66
  430.0 0.9 broadcast_in_dim.22
  430.8 3.5 all-to-all-start.7
  434.4 1.7 fusion.17
  436.2 5.1 all-to-all-done.7
  441.5 1.1 broadcast_in_dim.23
  442.6 10.9 %all-to-all-start.8 = ((f32[64,128,32]{1,2,0:T(8,128)}), f32[64,128,32]{1,2,0:T(8,128)S(1)}, u32[]{:S(2)}, u32[]{:S(2)}) async-start(f32[64,128,32]{1,2,0:T(8,128)} %broadcast_in_dim.23), calls=%async_computation.9 | async-start | bytes 2097152 | tf_op jit(solution)/shard_map/all_to_all | solution.py:11
  453.6 33.7 %psum.23 = f32[128]{0:T(128)} all-reduce(f32[128]{0:T(128)S(1)} %get-tuple-element.5), channel_id=1, replica_groups=mesh['batch'=4,'row'=4,'col'=16] {'batch'}, use_global_device_ids=true, to_apply=%region_9.10 | all-reduce | flops 128 | bytes 1024 | tf_op jit(solution)/shard_map/psum | solution.py:119
  487.3 3.0 fusion.6
  490.3 0.8 copy.71
  491.1 1.6 slice-done
  492.6 2.0 convolution_bitcast_fusion
  494.6 1.8 copy.72
  497.1 28.8 %all-reduce.5.cloned.1.call-done = f32[4096,128]{1,0:T(8,128)} async-done(((f32[4096,128]{1,0:T(8,128)}), f32[4096,128]{1,0:T(8,128)}) %all-reduce.5.cloned.1.call-update) | async-done | bytes 2097168 | tf_op jit(solution)/shard_map/psum | solution.py:119
  525.9 3.0 copy.87
  (48 shorter events, 3.3 us)
Async XLA Ops:
  7.2 226.5 %copy-start = (bf16[4096,128]{1,0:T(8,128)(2,1)S(1)}, bf16[4096,128]{1,0:T(8,128)(2,1)}, u32[]{:S(2)}) copy-start(bf16[4096,128]{1,0:T(8,128)(2,1)} %param.8) | copy-start | bytes 3145732
  7.2 7.0 %copy-start.7 = (bf16[128,8,128]{2,1,0:T(8,128)(2,1)S(1)}, bf16[128,8,128]{2,1,0:T(8,128)(2,1)}, u32[]{:S(2)}) copy-start(bf16[128,8,128]{2,1,0:T(8,128)(2,1)} %param.11) | copy-start | bytes 786436
  9.3 12.5 %all-to-all-start = ((f32[4,128,8,32]{1,3,2,0:T(8,128)}), f32[4,128,8,32]{1,3,2,0:T(8,128)S(1)}, u32[]{:S(2)}, u32[]{:S(2)}) async-start(f32[4,128,8,32]{1,3,2,0:T(8,128)} %broadcast_in_dim.16), calls=%async_computation | async-start | bytes 1048576 | tf_op jit(solution)/shard_map/all_to_all | solution.py:11
  14.2 199.5 %all-reduce.3.cloned.1.call-start = ((), (), s32[]{:S(2)}) async-start(), calls=%async_computation.10 | async-start | bytes 4194304 | tf_op jit(solution)/shard_map/psum | solution.py:91
  14.4 10.9 %copy-start.4 = (bf16[128,8,128]{0,2,1:T(8,128)(2,1)}, bf16[128,8,128]{0,2,1:T(8,128)(2,1)S(1)}, u32[]{:S(2)}) copy-start(bf16[128,8,128]{0,2,1:T(8,128)(2,1)S(1)} %copy.60) | copy-start | bytes 786436
  14.4 7.7 %copy-start.3 = (bf16[128,8,128]{2,1,0:T(8,128)(2,1)S(1)}, bf16[128,8,128]{2,1,0:T(8,128)(2,1)}, u32[]{:S(2)}) copy-start(bf16[128,8,128]{2,1,0:T(8,128)(2,1)} %param.6) | copy-start | bytes 786436
  30.0 186.4 %all-to-all-start.4 = ((f32[16,128,128]{2,1,0:T(8,128)}), f32[16,128,128]{2,1,0:T(8,128)}, u32[]{:S(2)}, u32[]{:S(2)}) async-start(f32[16,128,128]{2,1,0:T(8,128)} %convolution_bitcast_fusion.2), calls=%async_computation.4 | async-start | bytes 2097152 | tf_op jit(solution)/shard_map/all_to_all | solution.py:39
  213.7 15.5 %copy-start.1 = (f32[128,128,32]{1,2,0:T(8,128)S(1)}, f32[128,128,32]{1,2,0:T(8,128)}, u32[]{:S(2)}) copy-start(f32[128,128,32]{1,2,0:T(8,128)} %all-reduce.3.cloned.1.call-done) | copy-start | bytes 6291460
  217.0 7.4 %all-to-all-start.1 = ((f32[4,1,128]{2,1,0:T(1,128)}), f32[4,1,128]{2,1,0:T(1,128)S(1)}, u32[]{:S(2)}, u32[]{:S(2)}) async-start(f32[4,1,128]{2,1,0:T(1,128)} %broadcast_in_dim.17), calls=%async_computation.1 | async-start | bytes 4096 | tf_op jit(solution)/shard_map/all_to_all | solution.py:11
  225.1 10.3 %all-to-all-start.5 = ((f32[4,128,128]{2,1,0:T(8,128)}), f32[4,128,128]{2,1,0:T(8,128)}, u32[]{:S(2)}, u32[]{:S(2)}) async-start(f32[4,128,128]{2,1,0:T(8,128)} %broadcast_in_dim.20), calls=%async_computation.5 | async-start | bytes 524288 | tf_op jit(solution)/shard_map/all_to_all | solution.py:11
  233.7 15.0 %copy-start.8 = (f32[128]{0:T(128)S(1)}, f32[128]{0:T(128)}, u32[]{:S(2)}) copy-start(f32[128]{0:T(128)} %param.9) | copy-start | bytes 1540
  236.1 10.9 %all-to-all-start.2 = ((f32[4,128,128]{2,1,0:T(8,128)}), f32[4,128,128]{2,1,0:T(8,128)}, u32[]{:S(2)}, u32[]{:S(2)}) async-start(f32[4,128,128]{2,1,0:T(8,128)} %broadcast_in_dim.18), calls=%async_computation.2 | async-start | bytes 524288 | tf_op jit(solution)/shard_map/all_to_all | solution.py:11
  240.3 106.5 %reduce-scatter.2.cloned.1.call-start = ((), (), s32[]{:S(2)}) async-start(), calls=%async_computation.13 | async-start | bytes 2228224 | tf_op jit(solution)/shard_map/reduce_scatter | solution.py:62
  251.4 156.3 %all-gather.5.cloned.1.call-start = ((), (), s32[]{:S(2)}) async-start(), calls=%async_computation.14 | async-start | bytes 2228224 | tf_op jit(solution)/shard_map/all_gather | solution.py:63
  346.9 144.2 %all-gather.3.cloned.1.call-start = ((), (), s32[]{:S(2)}) async-start(), calls=%async_computation.11 | async-start | bytes 3932160 | tf_op jit(solution)/shard_map/all_gather | solution.py:45
  370.2 0.8 copy-start.5
  428.7 5.7 %copy-start.2 = (bf16[128,128,32]{0,2,1:T(8,128)(2,1)S(1)}, bf16[128,128,32]{0,2,1:T(8,128)(2,1)}, u32[]{:S(2)}) copy-start(bf16[128,128,32]{0,2,1:T(8,128)(2,1)} %copy.58) | copy-start | bytes 3145732
  430.8 10.4 %all-to-all-start.7 = ((f32[4,128,8,32]{1,3,2,0:T(8,128)}), f32[4,128,8,32]{1,3,2,0:T(8,128)S(1)}, u32[]{:S(2)}, u32[]{:S(2)}) async-start(f32[4,128,8,32]{1,3,2,0:T(8,128)} %broadcast_in_dim.22), calls=%async_computation.8 | async-start | bytes 1048576 | tf_op jit(solution)/shard_map/all_to_all | solution.py:11
  434.3 91.6 %all-reduce.5.cloned.1.call-start = ((), (), s32[]{:S(2)}) async-start(), calls=%async_computation.12 | async-start | bytes 4194304 | tf_op jit(solution)/shard_map/psum | solution.py:119
  436.1 51.2 %copy-start.6 = (bf16[16,128,128]{1,2,0:T(8,128)(2,1)S(1)}, bf16[16,128,128]{1,2,0:T(8,128)(2,1)}, u32[]{:S(2)}) copy-start(bf16[16,128,128]{1,2,0:T(8,128)(2,1)} %copy-done.5) | copy-start | bytes 1572868
  442.6 53.8 %all-to-all-start.8 = ((f32[64,128,32]{1,2,0:T(8,128)}), f32[64,128,32]{1,2,0:T(8,128)S(1)}, u32[]{:S(2)}, u32[]{:S(2)}) async-start(f32[64,128,32]{1,2,0:T(8,128)} %broadcast_in_dim.23), calls=%async_computation.9 | async-start | bytes 2097152 | tf_op jit(solution)/shard_map/all_to_all | solution.py:11
  491.1 1.6 slice-start
Sparse Core Ops, SparseCore 0:
  25.4 188.1 all-reduce.2
  251.5 95.3 reduce-scatter.1
  349.3 58.3 all-gather.4
  409.3 39.9 all-gather.2
  452.4 73.5 all-reduce.4
where the time goes:
time: 537 us; the launch traced here: 536 us
  waiting for transfers between devices  345 us (64%)
  blocking collectives  65 us (12%)
  starting transfers between devices  42.5 us (8%)
  local copies, waits for them, and re-layouts  31.8 us (6%)
  matrix products  22.6 us (4%)
  other arithmetic  14.9 us (3%)
  between operations  14 us (3%)
    psum x1, waiting for transfers between devices, local(): interact = lax.psum(partial_value, 'col')  172 us
    reduce_scatter x1, waiting for transfers between devices, sum_by_parts(): own = lax.psum_scatter(padded, axis, scatter_dimension=0, tiled=True)  95.4 us
    all_gather x1, waiting for transfers between devices, sum_by_parts(): whole = lax.all_gather(own, axis, axis=0, tiled=True)  34.7 us
    psum x1, blocking collectives, local(): lax.psum((contract_first(activated, d_pre_b), jnp.sum(d_preact, axis=0)),...  33.7 us
    all_to_all x2, blocking collectives, copy_for_each(): lax.all_to_all(jnp.broadcast_to(array[None], (size, *array.shape)), axis,...  31.3 us
    all_to_all x6, starting transfers between devices, copy_for_each(): lax.all_to_all(jnp.broadcast_to(array[None], (size, *array.shape)), axis,...  30.8 us
    psum x1, waiting for transfers between devices, local(): lax.psum((contract_first(activated, d_pre_b), jnp.sum(d_preact, axis=0)),...  28.8 us
    all_to_all x6, waiting for transfers between devices, copy_for_each(): lax.all_to_all(jnp.broadcast_to(array[None], (size, *array.shape)), axis,...  13.6 us
  transfers between devices with their start and end apart: 12, of which 7 were waited for; matrix products, arithmetic and copies ran while one was open for 10% of the time, Pallas kernels for 0%

commit v1 on v0

--- a/solution.py
+++ b/solution.py
@@ -88,7 +88,8 @@
         jnp.einsum("bde,ek->bdk", embeddings, own_proj, preferred_element_type=jnp.float32), "row"
     )
     partial_value = jnp.einsum("bde,bdk->bek", emb_float, folded, precision=highest)
-    interact = lax.psum(partial_value, "col")
+    blocks = lax.all_gather(partial_value, "col", axis=0, tiled=False)
+    interact = blocks.sum(axis=0)
     feature_count = emb_local * row_count * rank_cols
     square_sum = of_everyone(jnp.sum(interact * interact, axis=(1, 2)), "row")
     inv_rms = lax.rsqrt(square_sum / feature_count + epsilon)[:, None, None]

time: 537 us -> 748 us (1.39)
  waiting for transfers between devices: 345 us -> 551 us
  other arithmetic: 14.9 us -> 22.9 us
    all_gather x0 -> x1, waiting for transfers between devices: none -> 375 us  [local(): blocks = lax.all_gather(partial_value, 'col', axis=0, tiled=False)]
    psum x1 -> x0, waiting for transfers between devices: 172 us -> none  [local(): interact = lax.psum(partial_value, 'col')]
    reduce_sum x0 -> x1, other arithmetic: none -> 12.7 us  [local(): interact = blocks.sum(axis=0)]
    psum x1, waiting for transfers between devices: 28.8 us -> 38.6 us  [local(): lax.psum((contract_first(activated, d_pre_b), jnp.sum(d_preact, axis=0)),...]
  transfers between devices with their start and end apart: 12 -> 12, of which waited for: 7 -> 7; matrix products, arithmetic and copies ran while one was open for 10% -> 8% of each run, Pallas kernels for 0% -> 0%
where the time goes in v1:
time: 748 us; the launch traced here: 747 us
  waiting for transfers between devices  551 us (74%)
  blocking collectives  62.7 us (8%)
  starting transfers between devices  42.2 us (6%)
  local copies, waits for them, and re-layouts  31.7 us (4%)
  other arithmetic  22.9 us (3%)
  matrix products  22.3 us (3%)
  between operations  14 us (2%)
    all_gather x1, waiting for transfers between devices, local(): blocks = lax.all_gather(partial_value, 'col', axis=0, tiled=False)  375 us
    reduce_scatter x1, waiting for transfers between devices, sum_by_parts(): own = lax.psum_scatter(padded, axis, scatter_dimension=0, tiled=True)  88 us
    psum x1, waiting for transfers between devices, local(): lax.psum((contract_first(activated, d_pre_b), jnp.sum(d_preact, axis=0)),...  38.6 us
    all_gather x1, waiting for transfers between devices, sum_by_parts(): whole = lax.all_gather(own, axis, axis=0, tiled=True)  36.4 us
    all_to_all x2, blocking collectives, copy_for_each(): lax.all_to_all(jnp.broadcast_to(array[None], (size, *array.shape)), axis,...  36.2 us
    all_to_all x6, starting transfers between devices, copy_for_each(): lax.all_to_all(jnp.broadcast_to(array[None], (size, *array.shape)), axis,...  31.1 us
    psum x1, blocking collectives, local(): lax.psum((contract_first(activated, d_pre_b), jnp.sum(d_preact, axis=0)),...  26.5 us
  transfers between devices with their start and end apart: 12, of which 7 were waited for; matrix products, arithmetic and copies ran while one was open for 8% of the time, Pallas kernels for 0%

profile of v1, /device:TPU:1, one launch (start us, length us, event | category | flops | bytes accessed | tf_op | source)
XLA Modules:
  0.0 746.6 jit_solution(12240215444937441918)
XLA Ops:
  7.2 1.2 convolution_bitcast_fusion.4
  8.6 13.2 %all_to_all.47 = f32[4,128,8,32]{1,3,2,0:T(8,128)S(1)} all-to-all(f32[4,128,8,32]{1,3,2,0:T(8,128)S(1)} %broadcast_in_dim.16), channel_id=1, replica_groups=mesh['batch'=4,'row'=4,'col'=16] {'row'}, dimensions={0} | all-to-all | bytes 1048576 | tf_op jit(solution)/shard_map/all_to_all | solution.py:11
  22.1 3.2 convolution_bitcast_fusion.1
  25.6 7.4 dot_general.47
  33.0 4.7 convolution_bitcast_fusion.2
  37.6 11.0 %all-to-all-start.4 = ((f32[16,128,128]{2,1,0:T(8,128)}), f32[16,128,128]{2,1,0:T(8,128)}, u32[]{:S(2)}, u32[]{:S(2)}) async-start(f32[16,128,128]{2,1,0:T(8,128)} %convolution_bitcast_fusion.2), calls=%async_computation.4 | async-start | bytes 2097152 | tf_op jit(solution)/shard_map/all_to_all | solution.py:39
  48.6 374.5 %all-gather.9.cloned.1.call-done = f32[2048,128,32]{1,2,0:T(8,128)} async-done(((f32[128,128,32]{1,2,0:T(8,128)}), f32[2048,128,32]{1,2,0:T(8,128)}) %all-gather.9.cloned.1.call-update) | async-done | bytes 33554448 | tf_op jit(solution)/shard_map/all_gather | solution.py:91
  423.2 12.7 %reduce_sum.111 = f32[128,128,32]{1,2,0:T(8,128)S(1)} reduce(f32[16,128,128,32]{2,3,1,0:T(8,128)} %bitcast.51, f32[]{:T(128)} %constant.24.clone.1), dimensions={0}, to_apply=%region_1.0 | reduce | flops 7864320 | bytes 35651588 | tf_op jit(solution)/shard_map/reduce_sum | solution.py:92
  435.9 1.0 multiply_reduce_fusion.1
  437.5 3.9 all-to-all-start.1
  441.4 1.3 reduce_sum.116
  442.7 2.2 copy.55
  445.0 2.9 copy.57
  447.8 0.7 broadcast_in_dim.20
  448.6 4.2 all-to-all-start.5
  452.8 2.1 fusion.23
  454.9 3.5 all-to-all-done.5
  458.4 0.7 broadcast_in_dim.18
  459.2 4.0 all-to-all-start.2
  463.3 1.0 reduce_sum.117
  464.2 4.6 all-to-all-done.2
  468.8 1.6 reduce_sum.115
  470.4 0.9 fusion.24
  471.3 1.8 fusion.15
  473.1 88.0 %reduce-scatter.2.cloned.1.call-done = f32[8,4096]{1,0:T(8,128)} async-done(((f32[128,4096]{1,0:T(8,128)}), f32[8,4096]{1,0:T(8,128)}) %reduce-scatter.2.cloned.1.call-update) | async-done | bytes 131088 | tf_op jit(solution)/shard_map/reduce_scatter | solution.py:62
  561.4 23.0 %all_to_all.48 = bf16[16,128,128]{1,2,0:T(8,128)(2,1)S(1)} all-to-all(bf16[16,128,128]{1,2,0:T(8,128)(2,1)S(1)} %broadcast_in_dim.19), channel_id=1, replica_groups=mesh['batch'=4,'row'=4,'col'=16] {'col'}, dimensions={0} | all-to-all | bytes 1048576 | tf_op jit(solution)/shard_map/all_to_all | solution.py:11
  584.3 1.0 pad_maximum_fusion
  585.4 36.4 %all-gather.7.cloned.1.call-done = f32[128,4096]{1,0:T(8,128)} async-done(((f32[8,4096]{1,0:T(8,128)}), f32[128,4096]{1,0:T(8,128)}) %all-gather.7.cloned.1.call-update) | async-done | bytes 2097168 | tf_op jit(solution)/shard_map/all_gather | solution.py:63
  621.8 2.6 multiply_reduce_fusion
  625.0 4.3 all-to-all-start.6
  629.2 2.9 copy.61
  632.1 3.4 copy.63
  635.5 2.4 convolution_bitcast_fusion.3
  638.2 0.9 broadcast_in_dim.22
  639.0 4.2 all-to-all-start.7
  643.3 1.9 fusion.17
  645.2 5.0 all-to-all-done.7
  650.5 1.1 broadcast_in_dim.23
  651.7 10.4 %all-to-all-start.8 = ((f32[64,128,32]{1,2,0:T(8,128)}), f32[64,128,32]{1,2,0:T(8,128)S(1)}, u32[]{:S(2)}, u32[]{:S(2)}) async-start(f32[64,128,32]{1,2,0:T(8,128)} %broadcast_in_dim.23), calls=%async_computation.9 | async-start | bytes 2097152 | tf_op jit(solution)/shard_map/all_to_all | solution.py:11
  662.1 26.5 %psum.15 = f32[128]{0:T(128)} all-reduce(f32[128]{0:T(128)S(1)} %get-tuple-element.5), channel_id=1, replica_groups=mesh['batch'=4,'row'=4,'col'=16] {'batch'}, use_global_device_ids=true, to_apply=%region_9.10 | all-reduce | flops 128 | bytes 1024 | tf_op jit(solution)/shard_map/psum | solution.py:120
  688.6 2.9 fusion.6
  691.6 0.8 copy.69
  692.3 1.6 slice-done
  693.9 2.0 convolution_bitcast_fusion
  695.9 1.8 copy.70
  697.7 0.7 reduce_sum.122
  698.4 38.6 %all-reduce.2.cloned.1.call-done = f32[4096,128]{1,0:T(8,128)} async-done(((f32[4096,128]{1,0:T(8,128)}), f32[4096,128]{1,0:T(8,128)}) %all-reduce.2.cloned.1.call-update) | async-done | bytes 2097168 | tf_op jit(solution)/shard_map/psum | solution.py:120
  737.0 3.1 copy.84
  (51 shorter events, 2.8 us)
Async XLA Ops:
  7.2 445.7 %copy-start = (bf16[4096,128]{1,0:T(8,128)(2,1)S(1)}, bf16[4096,128]{1,0:T(8,128)(2,1)}, u32[]{:S(2)}) copy-start(bf16[4096,128]{1,0:T(8,128)(2,1)} %param.8) | copy-start | bytes 3145732
  7.2 14.9 %copy-start.3 = (bf16[128,8,128]{2,1,0:T(8,128)(2,1)S(1)}, bf16[128,8,128]{2,1,0:T(8,128)(2,1)}, u32[]{:S(2)}) copy-start(bf16[128,8,128]{2,1,0:T(8,128)(2,1)} %param.6) | copy-start | bytes 786436
  7.2 416.0 %all-gather.9.cloned.1.call-start = ((), (), s32[]{:S(2)}) async-start(), calls=%async_computation.14 | async-start | bytes 35651584 | tf_op jit(solution)/shard_map/all_gather | solution.py:91
  22.1 3.2 copy-start.8
  25.5 7.4 copy-start.4
  37.6 399.3 %all-to-all-start.4 = ((f32[16,128,128]{2,1,0:T(8,128)}), f32[16,128,128]{2,1,0:T(8,128)}, u32[]{:S(2)}, u32[]{:S(2)}) async-start(f32[16,128,128]{2,1,0:T(8,128)} %convolution_bitcast_fusion.2), calls=%async_computation.4 | async-start | bytes 2097152 | tf_op jit(solution)/shard_map/all_to_all | solution.py:39
  437.5 10.3 %all-to-all-start.1 = ((f32[4,1,128]{2,1,0:T(1,128)}), f32[4,1,128]{2,1,0:T(1,128)S(1)}, u32[]{:S(2)}, u32[]{:S(2)}) async-start(f32[4,1,128]{2,1,0:T(1,128)} %broadcast_in_dim.17), calls=%async_computation.1 | async-start | bytes 4096 | tf_op jit(solution)/shard_map/all_to_all | solution.py:11
  448.6 9.9 %all-to-all-start.5 = ((f32[4,128,128]{2,1,0:T(8,128)}), f32[4,128,128]{2,1,0:T(8,128)}, u32[]{:S(2)}, u32[]{:S(2)}) async-start(f32[4,128,128]{2,1,0:T(8,128)} %broadcast_in_dim.20), calls=%async_computation.5 | async-start | bytes 524288 | tf_op jit(solution)/shard_map/all_to_all | solution.py:11
  452.8 17.6 %copy-start.9 = (f32[128]{0:T(128)S(1)}, f32[128]{0:T(128)}, u32[]{:S(2)}) copy-start(f32[128]{0:T(128)} %param.9) | copy-start | bytes 1540
  459.2 9.6 %all-to-all-start.2 = ((f32[4,128,128]{2,1,0:T(8,128)}), f32[4,128,128]{2,1,0:T(8,128)}, u32[]{:S(2)}, u32[]{:S(2)}) async-start(f32[4,128,128]{2,1,0:T(8,128)} %broadcast_in_dim.18), calls=%async_computation.2 | async-start | bytes 524288 | tf_op jit(solution)/shard_map/all_to_all | solution.py:11
  463.2 97.9 %reduce-scatter.2.cloned.1.call-start = ((), (), s32[]{:S(2)}) async-start(), calls=%async_computation.12 | async-start | bytes 2228224 | tf_op jit(solution)/shard_map/reduce_scatter | solution.py:62
  473.0 111.3 %copy-start.5 = (bf16[128,8,128]{0,2,1:T(8,128)(2,1)S(1)}, bf16[128,8,128]{0,2,1:T(8,128)(2,1)}, u32[]{:S(2)}) copy-start(bf16[128,8,128]{0,2,1:T(8,128)(2,1)} %copy-done.4) | copy-start | bytes 786436
  473.1 148.7 %all-gather.7.cloned.1.call-start = ((), (), s32[]{:S(2)}) async-start(), calls=%async_computation.13 | async-start | bytes 2228224 | tf_op jit(solution)/shard_map/all_gather | solution.py:63
  561.1 131.2 %all-gather.5.cloned.1.call-start = ((), (), s32[]{:S(2)}) async-start(), calls=%async_computation.10 | async-start | bytes 3932160 | tf_op jit(solution)/shard_map/all_gather | solution.py:45
  584.3 40.1 %copy-start.6 = (bf16[16,128,128]{1,2,0:T(8,128)(2,1)}, bf16[16,128,128]{1,2,0:T(8,128)(2,1)S(1)}, u32[]{:S(2)}) copy-start(bf16[16,128,128]{1,2,0:T(8,128)(2,1)S(1)} %all_to_all.48) | copy-start | bytes 1572868
  625.0 10.5 %all-to-all-start.6 = ((f32[4,1,128]{2,1,0:T(1,128)}), f32[4,1,128]{2,1,0:T(1,128)S(1)}, u32[]{:S(2)}, u32[]{:S(2)}) async-start(f32[4,1,128]{2,1,0:T(1,128)} %broadcast_in_dim.21), calls=%async_computation.7 | async-start | bytes 4096 | tf_op jit(solution)/shard_map/all_to_all | solution.py:11
  637.9 5.4 copy-start.2
  639.0 11.2 %all-to-all-start.7 = ((f32[4,128,8,32]{1,3,2,0:T(8,128)}), f32[4,128,8,32]{1,3,2,0:T(8,128)S(1)}, u32[]{:S(2)}, u32[]{:S(2)}) async-start(f32[4,128,8,32]{1,3,2,0:T(8,128)} %broadcast_in_dim.22), calls=%async_computation.8 | async-start | bytes 1048576 | tf_op jit(solution)/shard_map/all_to_all | solution.py:11
  643.3 93.7 %all-reduce.2.cloned.1.call-start = ((), (), s32[]{:S(2)}) async-start(), calls=%async_computation.11 | async-start | bytes 4194304 | tf_op jit(solution)/shard_map/psum | solution.py:120
  645.2 43.4 %copy-start.7 = (bf16[16,128,128]{1,2,0:T(8,128)(2,1)S(1)}, bf16[16,128,128]{1,2,0:T(8,128)(2,1)}, u32[]{:S(2)}) copy-start(bf16[16,128,128]{1,2,0:T(8,128)(2,1)} %copy-done.6) | copy-start | bytes 1572868
  651.7 46.0 %all-to-all-start.8 = ((f32[64,128,32]{1,2,0:T(8,128)}), f32[64,128,32]{1,2,0:T(8,128)S(1)}, u32[]{:S(2)}, u32[]{:S(2)}) async-start(f32[64,128,32]{1,2,0:T(8,128)} %broadcast_in_dim.23), calls=%async_computation.9 | async-start | bytes 2097152 | tf_op jit(solution)/shard_map/all_to_all | solution.py:11
  692.3 1.6 slice-start
  737.0 3.1 copy-start.1
Sparse Core Ops, SparseCore 0:
  25.4 397.7 all-gather.8
  473.2 87.8 reduce-scatter.1
  563.5 58.2 all-gather.6
  623.5 39.9 all-gather.4
  666.6 70.3 all-reduce.1
